TPU v7x, 128 devices: a whole 4x4x4 slice. The times are simulated.
128 devices in a mesh: dp: 8 (over z, x_hi), mp: 16 (over y, x_lo, core).
Axes of the slice: x: 4 (x_hi: 2, x_lo: 2; x = x_hi * 2 + x_lo), y: 4, z: 4, core: 2. Of those that a mesh axis runs over, the one named last changes fastest.
Arguments:
- tokens: bfloat16 [16384, 2048], P(('dp', 'mp')), may hold values from -6 to 6
- attn_gain: float32 [2048], replicated, may hold values from 0.25 to 1.75
- mlp_gain: float32 [2048], replicated, may hold values from 0.25 to 1.75
- query_weight: bfloat16 [2048, 2048], replicated, as said below
- keyval_weight: bfloat16 [2048, 1024], replicated, as said below
- output_weight: bfloat16 [2048, 2048], replicated, may hold values from -0.125 to 0.125
- gate_rows: float32 [2048, 8192], P(('dp', 'mp')), may hold values from -0.125 to 0.125
- up_rows: float32 [2048, 8192], P(('dp', 'mp')), may hold values from -0.125 to 0.125
- down_rows: float32 [8192, 2048], P(('dp', 'mp')), may hold values from -0.0625 to 0.0625
- lengths: int32 [8, 1], P('dp'), may hold values from 1024 to 2048
- valid: int32 [16384], P(('dp', 'mp')), may hold values 0 or 1
- page_table: int32 [1024, 1], P(('dp', 'mp')), may hold values from 0 to 7; in each aligned block of 8 rows (0 to 7, 8 to 15, ...) at most 2 rows name the same one
Outputs:
- layer_out: bfloat16 [16384, 2048], P(('dp', 'mp'))
- page_cache: bfloat16 [8, 16, 8, 2, 16, 1024], P('dp', 'mp')
Inputs may be any that keep to these rules, and one draw needn't show every extreme that they name: `page_table`: of the 8 pages of one device at most 2 name the same holder; in every draw some device sends 2 pages to one holder. `query_weight`: entries are independent, of mean zero. `keyval_weight`: entries are independent, of mean zero.
All inputs are finite; a program needn't handle non-finite values. No bound on the sum of `valid` on one device may be relied on, other than what follows from the above.
Results may differ from a plain program's by a relative error of at most 0.02.
The roundings to bfloat16 on the way count: a program that leaves them out, or rounds other values in their place, can miss the bound.
Values may be sent and summed in bfloat16 or wider, within the bound.
A program may use at most 128 MiB of HBM per device.

v0:
```python
import jax
import jax.numpy as jnp
from jax import lax
from jax.sharding import PartitionSpec as P

QH = 32
KVH = 8
HD = 64
PAGE = 16
PAGE_MOST = 2
rope_base = 500000.0


def rms_scale(values, gain):
    mean_square = jnp.mean(values * values, axis=-1, keepdims=True)
    return values * lax.rsqrt(mean_square + 1e-05) * gain


def prompt_ids(lens, rows):
    ends = jnp.cumsum(lens)
    starts = ends - lens
    segment = jnp.sum((rows[:, None] >= ends[None, :]).astype(jnp.int32), axis=1)
    prompt_range = jnp.arange(lens.shape[0], dtype=jnp.int32)
    first = jnp.sum(
        jnp.where(segment[:, None] == prompt_range[None, :], starts[None, :], 0), axis=1
    )
    return (segment, rows - first)


def rotate(heads, position):
    half = heads.shape[-1] // 2
    expo = jnp.arange(half, dtype=jnp.float32) * (2.0 / heads.shape[-1])
    inverse = jnp.exp(-expo * jnp.log(jnp.float32(rope_base)))
    angle = position.astype(jnp.float32)[:, None] * inverse[None, :]
    cosine = jnp.cos(angle)[:, None, :]
    sine = jnp.sin(angle)[:, None, :]
    first_half = heads[..., :half]
    second_half = heads[..., half:]
    return jnp.concatenate(
        [first_half * cosine - second_half * sine, second_half * cosine + first_half * sine],
        axis=-1,
    )


def on_device(
    tokens,
    attn_gain,
    mlp_gain,
    query_weight,
    keyval_weight,
    output_weight,
    gate_rows,
    up_rows,
    down_rows,
    lengths,
    valid,
    page_table,
):
    mp_count = lax.axis_size("mp")
    dp_count = lax.axis_size("dp")
    column = lax.axis_index("mp")
    tok_dev = tokens.shape[0]
    tok_grp = tok_dev * mp_count
    heads_dev = QH // mp_count
    lens = lengths[0]
    local_rows = column * tok_dev + jnp.arange(tok_dev, dtype=jnp.int32)
    unused_segment, position = prompt_ids(lens, local_rows)
    tokens_f = tokens.astype(jnp.float32)
    normed = rms_scale(tokens_f, attn_gain).astype(jnp.bfloat16)
    queries = jnp.dot(normed, query_weight, preferred_element_type=jnp.float32).reshape(
        tok_dev, QH, HD
    )
    queries = rotate(queries, position).astype(jnp.bfloat16)
    keyval = jnp.dot(normed, keyval_weight, preferred_element_type=jnp.float32)
    keys = rotate(keyval[:, : KVH * HD].reshape(tok_dev, KVH, HD), position).astype(jnp.bfloat16)
    values = keyval[:, KVH * HD :].reshape(tok_dev, KVH, HD).astype(jnp.bfloat16)
    query_send = queries.reshape(tok_dev, mp_count, heads_dev * HD)
    pair_send = jnp.repeat(jnp.concatenate([keys, values], axis=-1), mp_count // KVH, axis=1)
    flag_send = jnp.broadcast_to(valid.astype(jnp.bfloat16)[:, None, None], (tok_dev, mp_count, 1))
    query_in, pair_in, flag_in = (
        lax.all_to_all(query_send, "mp", split_axis=1, concat_axis=0, tiled=True),
        lax.all_to_all(pair_send, "mp", split_axis=1, concat_axis=0, tiled=True),
        lax.all_to_all(flag_send, "mp", split_axis=1, concat_axis=0, tiled=True),
    )
    query_in = query_in.reshape(tok_grp, heads_dev, HD)
    key_in = pair_in[:, 0, :HD]
    value_in = pair_in[:, 0, HD:]
    key_open = flag_in[:, 0, 0] > 0.5
    group_rows = jnp.arange(tok_grp, dtype=jnp.int32)
    segment_all, unused_position = prompt_ids(lens, group_rows)
    block_rows = min(512, tok_grp)

    def attend_block(block_index):
        start = block_index * block_rows
        query_block = lax.dynamic_slice_in_dim(query_in, start, block_rows, 0)
        query_rows = start + jnp.arange(block_rows, dtype=jnp.int32)
        query_segment = lax.dynamic_slice_in_dim(segment_all, start, block_rows, 0)
        scores = (
            jnp.einsum("thd,sd->hts", query_block, key_in, preferred_element_type=jnp.float32)
            * 0.125
        )
        allowed = (
            (query_segment[:, None] == segment_all[None, :])
            & (group_rows[None, :] <= query_rows[:, None])
            & (key_open[None, :] | (group_rows[None, :] == query_rows[:, None]))
        )
        scores = jnp.where(allowed[None], scores, jnp.float32(-1e30))
        top = jnp.max(scores, axis=-1, keepdims=True)
        expd = jnp.exp(scores - top)
        weights = (expd / jnp.sum(expd, axis=-1, keepdims=True)).astype(jnp.bfloat16)
        mixed = jnp.einsum("hts,sd->thd", weights, value_in, preferred_element_type=jnp.float32)
        return mixed.astype(jnp.bfloat16).reshape(block_rows, heads_dev * HD)

    attended = lax.map(attend_block, jnp.arange(tok_grp // block_rows, dtype=jnp.int32))
    attended = attended.reshape(tok_grp, heads_dev * HD)
    attended_back = lax.all_to_all(attended, "mp", split_axis=0, concat_axis=1, tiled=True)
    hidden_state = (
        tokens_f + jnp.dot(attended_back, output_weight, preferred_element_type=jnp.float32)
    ).astype(jnp.bfloat16)
    hidden_f = hidden_state.astype(jnp.float32)
    mlp_in = rms_scale(hidden_f, mlp_gain).astype(jnp.bfloat16)
    mlp_group = lax.all_gather(mlp_in, "mp", axis=0, tiled=True)
    rows_dev = gate_rows.shape[0]
    block_width = gate_rows.shape[1] // (dp_count * mp_count)

    def arrange(weight_rows):
        shaped = weight_rows.astype(jnp.bfloat16).reshape(rows_dev, dp_count, mp_count, block_width)
        return jnp.transpose(shaped, (0, 2, 1, 3)).reshape(
            rows_dev, mp_count, dp_count * block_width
        )

    gate_piece, up_piece = (
        lax.all_to_all(arrange(gate_rows), "mp", split_axis=1, concat_axis=0, tiled=True),
        lax.all_to_all(arrange(up_rows), "mp", split_axis=1, concat_axis=0, tiled=True),
    )
    gate_piece = gate_piece.reshape(rows_dev * mp_count, dp_count * block_width)
    up_piece = up_piece.reshape(rows_dev * mp_count, dp_count * block_width)
    gate_block, up_block = (
        lax.all_gather(gate_piece, "dp", axis=0, tiled=True),
        lax.all_gather(up_piece, "dp", axis=0, tiled=True),
    )
    gate = jnp.dot(mlp_group, gate_block, preferred_element_type=jnp.float32)
    upper = jnp.dot(mlp_group, up_block, preferred_element_type=jnp.float32)
    activated = (jax.nn.silu(gate) * upper).astype(jnp.bfloat16)
    down_block = lax.all_gather(down_rows.astype(jnp.bfloat16), "dp", axis=0, tiled=True)
    mlp_sum = lax.psum_scatter(
        jnp.dot(activated, down_block, preferred_element_type=jnp.float32).astype(jnp.bfloat16),
        "mp",
        scatter_dimension=0,
        tiled=True,
    ).astype(jnp.float32)
    layer_out = (hidden_f + mlp_sum).astype(jnp.bfloat16)
    pages_dev = tok_dev // PAGE
    feature = 2 * KVH * HD
    cache_rows = jnp.concatenate(
        [keys.reshape(tok_dev, KVH * HD), values.reshape(tok_dev, KVH * HD)], axis=1
    )
    holders = page_table[:, 0]
    order = jnp.arange(pages_dev, dtype=jnp.int32)
    same_earlier = (holders[None, :] == holders[:, None]) & (order[None, :] < order[:, None])
    rank = jnp.sum(same_earlier.astype(jnp.int32), axis=1)
    target = holders * PAGE_MOST + rank
    slot_range = jnp.arange(dp_count * PAGE_MOST, dtype=jnp.int32)
    placing = (slot_range[:, None] == target[None, :]).astype(jnp.bfloat16)
    flat_pages = cache_rows.reshape(pages_dev, PAGE * feature)
    page_send = jnp.dot(placing, flat_pages, preferred_element_type=jnp.float32).astype(
        jnp.bfloat16
    )
    page_send = page_send.reshape(dp_count, PAGE_MOST, PAGE, feature)
    received = lax.all_to_all(page_send, "dp", split_axis=0, concat_axis=0, tiled=True)
    page_cache = received[None, None]
    return (layer_out, page_cache)


def solution(mesh):
    return jax.shard_map(
        on_device,
        mesh=mesh,
        in_specs=(
            P(("dp", "mp"), None),
            P(),
            P(),
            P(),
            P(),
            P(),
            P(("dp", "mp"), None),
            P(("dp", "mp"), None),
            P(("dp", "mp"), None),
            P("dp", None),
            P(("dp", "mp")),
            P(("dp", "mp"), None),
        ),
        out_specs=(P(("dp", "mp"), None), P("dp", "mp", None, None, None, None)),
        check_vma=False,
    )
```

profile of v0, /device:TPU:4, one launch (start us, length us, event | category | flops | bytes accessed | tf_op | source)
XLA Modules:
  0.0 442.2 jit_solution(11806712546734390694)
XLA Ops:
  8.5 5.2 %all-to-all-start = ((bf16[128,16,1]{0,2,1:T(2,128)(2,1)}), bf16[128,16,1]{0,2,1:T(2,128)(2,1)S(1)}, u32[]{:S(2)}, u32[]{:S(2)}) async-start(bf16[128,16,1]{0,2,1:T(2,128)(2,1)} %broadcast_in_dim.28), calls=%async_computation | async-start | bytes 16384 | tf_op jit(solution)/shard_map/all_to_all | solution.py:83
  20.4 5.7 %all-to-all-start.4 = ((bf16[16,16,512]{2,0,1:T(8,128)(2,1)}), bf16[16,16,512]{2,0,1:T(8,128)(2,1)S(1)}, u32[]{:S(2)}, u32[]{:S(2)}) async-start(bf16[16,16,512]{2,0,1:T(8,128)(2,1)} %copy.77), calls=%async_computation.4 | async-start | bytes 524288 | tf_op jit(solution)/shard_map/all_to_all | solution.py:133
  26.3 7.8 %all-to-all-done.4 = bf16[16,16,512]{2,0,1:T(8,128)(2,1)S(1)} async-done(((bf16[16,16,512]{2,0,1:T(8,128)(2,1)}), bf16[16,16,512]{2,0,1:T(8,128)(2,1)S(1)}, u32[]{:S(2)}, u32[]{:S(2)}) %all-to-all-start.4) | async-done | bytes 262176 | tf_op jit(solution)/shard_map/all_to_all | solution.py:133
  38.6 6.8 %fusion.42 = f32[128,2048]{0,1:T(8,128)S(1)} fusion(bf16[2048,2048]{1,0:T(8,128)(2,1)} %param.17, bf16[128,2048]{1,0:T(8,128)(2,1)S(1)} %copy-done, f32[2048]{0:T(1024)S(1)} %copy-done.6, f32[128]{0:T(128)S(1)} %add_rsqrt_fusion.1), kind=kOutput, calls=%fused_computation.57 | convolution fusion | flops 1074790400 | bytes 9970176 | tf_op jit(solution)/shard_map/dot_general | solution.py:70
  55.6 8.3 %all-to-all-done.1 = bf16[128,16,128]{0,2,1:T(8,128)(2,1)S(1)} async-done(((bf16[128,16,128]{0,2,1:T(8,128)(2,1)}), bf16[128,16,128]{0,2,1:T(8,128)(2,1)S(1)}, u32[]{:S(2)}, u32[]{:S(2)}) %all-to-all-start.1) | async-done | bytes 524320 | tf_op jit(solution)/shard_map/all_to_all | solution.py:81
  64.5 68.7 %while.12 = (s32[]{:T(128)}, bf16[4,512,128]{2,1,0:T(8,128)(2,1)S(1)}, s32[4]{0:T(128)S(1)}, s32[2048]{0:T(1024)S(1)}, pred[2048]{0:T(1024)(128)(4,1)S(1)}, /*in...) while((s32[]{:T(128)}, ...), condition=%wide.region_4.5_spmd.clone.clone, body=%wide.region_1.0_spmd.clone.clone.sunk | while | flops 555813376 | bytes 20213952 | solution.py:114
  69.4 7.2 %fusion.78 = (f32[2,512]{1,0:T(2,128)S(1)}, f32[2,512,2048]{2,1,0:T(8,128)}) fusion(pred[512,2048]{1,0:T(8,128)(4,1)S(1)} %fusion.77, bf16[2048,64]{0,1:T(8,128)(2,1)} %get-tuple-element.220, bf16[2048,2,64]{0,2,1:T(8,128)(2,1)S(1)} %get-tuple-element.219, s32[]{:T(128)S(6)} %select_n.41), kind=kOutput, calls=%fused_computation.76.clone.1 | convolution fusion | flops 276826112 | bytes 9834500 | tf_op jit(solution)/shard_map/while/body/eval_jaxpr/sub | solution.py:109
  76.6 4.9 %fusion.79 = bf16[2,512,64]{1,2,0:T(8,128)(2,1)S(1)} fusion(f32[2,512,2048]{2,1,0:T(8,128)} %get-tuple-element.188, f32[2,512]{1,0:T(2,128)S(1)} %get-tuple-element.189, bf16[2048,64]{0,1:T(8,128)(2,1)S(1)} %get-tuple-element.221), kind=kOutput, calls=%fused_computation.17.clone.1 | convolution fusion | flops 272695296 | bytes 8785920 | tf_op jit(solution)/shard_map/while/body/eval_jaxpr/hts,sd->thd/dot_general | solution.py:111
  86.6 7.2 %fusion.78 = (f32[2,512]{1,0:T(2,128)S(1)}, f32[2,512,2048]{2,1,0:T(8,128)}) fusion(pred[512,2048]{1,0:T(8,128)(4,1)S(1)} %fusion.77, bf16[2048,64]{0,1:T(8,128)(2,1)} %get-tuple-element.220, bf16[2048,2,64]{0,2,1:T(8,128)(2,1)S(1)} %get-tuple-element.219, s32[]{:T(128)S(6)} %select_n.41), kind=kOutput, calls=%fused_computation.76.clone.1 | convolution fusion | flops 276826112 | bytes 9834500 | tf_op jit(solution)/shard_map/while/body/eval_jaxpr/sub | solution.py:109
  93.8 4.9 %fusion.79 = bf16[2,512,64]{1,2,0:T(8,128)(2,1)S(1)} fusion(f32[2,512,2048]{2,1,0:T(8,128)} %get-tuple-element.188, f32[2,512]{1,0:T(2,128)S(1)} %get-tuple-element.189, bf16[2048,64]{0,1:T(8,128)(2,1)S(1)} %get-tuple-element.221), kind=kOutput, calls=%fused_computation.17.clone.1 | convolution fusion | flops 272695296 | bytes 8785920 | tf_op jit(solution)/shard_map/while/body/eval_jaxpr/hts,sd->thd/dot_general | solution.py:111
  103.8 7.2 %fusion.78 = (f32[2,512]{1,0:T(2,128)S(1)}, f32[2,512,2048]{2,1,0:T(8,128)}) fusion(pred[512,2048]{1,0:T(8,128)(4,1)S(1)} %fusion.77, bf16[2048,64]{0,1:T(8,128)(2,1)} %get-tuple-element.220, bf16[2048,2,64]{0,2,1:T(8,128)(2,1)S(1)} %get-tuple-element.219, s32[]{:T(128)S(6)} %select_n.41), kind=kOutput, calls=%fused_computation.76.clone.1 | convolution fusion | flops 276826112 | bytes 9834500 | tf_op jit(solution)/shard_map/while/body/eval_jaxpr/sub | solution.py:109
  111.0 4.8 %fusion.79 = bf16[2,512,64]{1,2,0:T(8,128)(2,1)S(1)} fusion(f32[2,512,2048]{2,1,0:T(8,128)} %get-tuple-element.188, f32[2,512]{1,0:T(2,128)S(1)} %get-tuple-element.189, bf16[2048,64]{0,1:T(8,128)(2,1)S(1)} %get-tuple-element.221), kind=kOutput, calls=%fused_computation.17.clone.1 | convolution fusion | flops 272695296 | bytes 8785920 | tf_op jit(solution)/shard_map/while/body/eval_jaxpr/hts,sd->thd/dot_general | solution.py:111
  121.0 7.2 %fusion.78 = (f32[2,512]{1,0:T(2,128)S(1)}, f32[2,512,2048]{2,1,0:T(8,128)}) fusion(pred[512,2048]{1,0:T(8,128)(4,1)S(1)} %fusion.77, bf16[2048,64]{0,1:T(8,128)(2,1)} %get-tuple-element.220, bf16[2048,2,64]{0,2,1:T(8,128)(2,1)S(1)} %get-tuple-element.219, s32[]{:T(128)S(6)} %select_n.41), kind=kOutput, calls=%fused_computation.76.clone.1 | convolution fusion | flops 276826112 | bytes 9834500 | tf_op jit(solution)/shard_map/while/body/eval_jaxpr/sub | solution.py:109
  128.1 4.8 %fusion.79 = bf16[2,512,64]{1,2,0:T(8,128)(2,1)S(1)} fusion(f32[2,512,2048]{2,1,0:T(8,128)} %get-tuple-element.188, f32[2,512]{1,0:T(2,128)S(1)} %get-tuple-element.189, bf16[2048,64]{0,1:T(8,128)(2,1)S(1)} %get-tuple-element.221), kind=kOutput, calls=%fused_computation.17.clone.1 | convolution fusion | flops 272695296 | bytes 8785920 | tf_op jit(solution)/shard_map/while/body/eval_jaxpr/hts,sd->thd/dot_general | solution.py:111
  133.1 13.5 %all_to_all.96 = bf16[16,128,128]{2,1,0:T(8,128)(2,1)S(1)} all-to-all(bf16[16,128,128]{2,1,0:T(8,128)(2,1)S(1)} %bitcast.125), channel_id=1, replica_groups=mesh['dp'=8,'mp'=16] {'mp'}, dimensions={0} | all-to-all | bytes 1048576 | tf_op jit(solution)/shard_map/all_to_all | solution.py:116
  147.0 4.8 %multiply_reduce_fusion = (f32[128]{0:T(128)S(1)}, f32[128,2048]{1,0:T(8,128)S(1)}) fusion(bf16[128,2048]{0,1:T(8,128)(2,1)S(1)} %bitcast.112, bf16[2048,2048]{1,0:T(8,128)(2,1)} %param.19, bf16[128,2048]{1,0:T(8,128)(2,1)S(1)} %copy-done), kind=kOutput, calls=%fused_computation.44 | convolution fusion | flops 1075314560 | bytes 10486272 | tf_op jit(solution)/shard_map/dot_general | solution.py:118
  154.9 11.8 %all_to_all.97 = bf16[16,16,512]{2,0,1:T(8,128)(2,1)} all-to-all(bf16[16,16,512]{2,0,1:T(8,128)(2,1)S(1)} %copy.79), channel_id=1, replica_groups=mesh['dp'=8,'mp'=16] {'mp'}, dimensions={1} | all-to-all | bytes 524288 | tf_op jit(solution)/shard_map/all_to_all | solution.py:134
  167.0 38.3 %all-gather.5.cloned.1.call-done = bf16[2048,2048]{1,0:T(8,128)(2,1)} async-done(((bf16[128,2048]{1,0:T(8,128)(2,1)}), bf16[2048,2048]{1,0:T(8,128)(2,1)}) %all-gather.5.cloned.1.call-update) | async-done | bytes 8388624 | tf_op jit(solution)/shard_map/all_gather | solution.py:122
  205.3 10.4 %fusion.57 = f32[2048,512]{1,0:T(8,128)} fusion(bf16[2048,2048]{1,0:T(8,128)(2,1)} %all-gather.5.cloned.1.call-done, bf16[2048,512]{1,0:T(8,128)(2,1)} %all-gather.7.cloned.1.call-done), kind=kOutput, calls=%fused_computation.77 | convolution fusion | flops 4294967296 | bytes 14680064 | tf_op jit(solution)/shard_map/dot_general | solution.py:142
  215.7 45.8 %all-gather.11.cloned.1.call-done = bf16[512,2048]{1,0:T(8,128)(2,1)} async-done(((bf16[64,2048]{1,0:T(8,128)(2,1)}), bf16[512,2048]{1,0:T(8,128)(2,1)}) %all-gather.11.cloned.1.call-update) | async-done | bytes 2097168 | tf_op jit(solution)/shard_map/all_gather | solution.py:145
  261.5 54.1 %all-gather.9.cloned.1.call-done = bf16[2048,512]{1,0:T(8,128)(2,1)} async-done(((bf16[256,512]{1,0:T(8,128)(2,1)}), bf16[2048,512]{1,0:T(8,128)(2,1)}) %all-gather.9.cloned.1.call-update) | async-done | bytes 2097168 | tf_op jit(solution)/shard_map/all_gather | solution.py:140
  315.6 15.2 %convolution_convert_fusion.1 = bf16[2048,2048]{1,0:T(8,128)(2,1)} fusion(bf16[512,2048]{1,0:T(8,128)(2,1)} %all-gather.11.cloned.1.call-done, f32[2048,512]{1,0:T(8,128)} %fusion.57, bf16[2048,2048]{1,0:T(8,128)(2,1)} %all-gather.5.cloned.1.call-done, bf16[2048,512]{1,0:T(8,128)(2,1)} %all-gather.9.cloned.1.call-done), kind=kOutput, calls=%fused_computation.32 | convolution fusion | flops 8600420352 | bytes 25165824 | tf_op jit(solution)/shard_map/dot_general | solution.py:147
  332.3 18.0 %all_to_all.98 = bf16[8,2,16,1024]{3,2,1,0:T(8,128)(2,1)S(1)} all-to-all(bf16[8,2,16,1024]{3,2,1,0:T(8,128)(2,1)S(1)} %bitcast.120), channel_id=1, replica_groups=mesh['dp'=8,'mp'=16] {'dp'}, dimensions={0} | all-to-all | bytes 1048576 | tf_op jit(solution)/shard_map/all_to_all | solution.py:170
  350.3 82.7 %reduce-scatter.2.cloned.1.call-done = bf16[128,2048]{1,0:T(8,128)(2,1)} async-done(((bf16[2048,2048]{1,0:T(8,128)(2,1)}), bf16[128,2048]{1,0:T(8,128)(2,1)}) %reduce-scatter.2.cloned.1.call-update) | async-done | bytes 524304 | tf_op jit(solution)/shard_map/reduce_scatter | solution.py:146
  (108 shorter events, 48.0 us)
Async XLA Ops:
  7.2 11.3 %copy-start.2 = (f32[16,8192]{1,0:T(8,128)S(1)}, f32[16,8192]{1,0:T(8,128)}, u32[]{:S(2)}) copy-start(f32[16,8192]{1,0:T(8,128)} %param.20) | copy-start | bytes 1572868
  8.5 11.9 %all-to-all-start = ((bf16[128,16,1]{0,2,1:T(2,128)(2,1)}), bf16[128,16,1]{0,2,1:T(2,128)(2,1)S(1)}, u32[]{:S(2)}, u32[]{:S(2)}) async-start(bf16[128,16,1]{0,2,1:T(2,128)(2,1)} %broadcast_in_dim.28), calls=%async_computation | async-start | bytes 16384 | tf_op jit(solution)/shard_map/all_to_all | solution.py:83
  18.3 20.3 %copy-start = (bf16[128,2048]{1,0:T(8,128)(2,1)S(1)}, bf16[128,2048]{1,0:T(8,128)(2,1)}, u32[]{:S(2)}) copy-start(bf16[128,2048]{1,0:T(8,128)(2,1)} %param.14) | copy-start | bytes 1572868
  18.3 20.3 %copy-start.6 = (f32[2048]{0:T(1024)S(1)}, f32[2048]{0:T(1024)}, u32[]{:S(2)}) copy-start(f32[2048]{0:T(1024)} %param.15) | copy-start | bytes 24580
  20.4 13.8 %all-to-all-start.4 = ((bf16[16,16,512]{2,0,1:T(8,128)(2,1)}), bf16[16,16,512]{2,0,1:T(8,128)(2,1)S(1)}, u32[]{:S(2)}, u32[]{:S(2)}) async-start(bf16[16,16,512]{2,0,1:T(8,128)(2,1)} %copy.77), calls=%async_computation.4 | async-start | bytes 524288 | tf_op jit(solution)/shard_map/all_to_all | solution.py:133
  34.1 11.3 %copy-start.1 = (bf16[16,16,512]{2,0,1:T(8,128)(2,1)}, bf16[16,16,512]{2,0,1:T(8,128)(2,1)S(1)}, u32[]{:S(2)}) copy-start(bf16[16,16,512]{2,0,1:T(8,128)(2,1)S(1)} %all-to-all-done.4) | copy-start | bytes 786436
  35.0 14.4 %all-to-all-start.2 = ((bf16[128,16,128]{0,2,1:T(8,128)(2,1)}), bf16[128,16,128]{0,2,1:T(8,128)(2,1)S(1)}, u32[]{:S(2)}, u32[]{:S(2)}) async-start(bf16[128,16,128]{0,2,1:T(8,128)(2,1)} %bitcast.10), calls=%async_computation.2 | async-start | bytes 1048576 | tf_op jit(solution)/shard_map/all_to_all | solution.py:82
  47.1 17.3 %copy-start.5 = (bf16[4,512,128]{2,1,0:T(8,128)(2,1)S(1)}, bf16[4,512,128]{2,1,0:T(8,128)(2,1)}, u32[]{:S(2)}) copy-start(bf16[4,512,128]{2,1,0:T(8,128)(2,1)} %custom-call) | copy-start | bytes 1572868
  49.4 14.4 %all-to-all-start.1 = ((bf16[128,16,128]{0,2,1:T(8,128)(2,1)}), bf16[128,16,128]{0,2,1:T(8,128)(2,1)S(1)}, u32[]{:S(2)}, u32[]{:S(2)}) async-start(bf16[128,16,128]{0,2,1:T(8,128)(2,1)} %bitcast.5), calls=%async_computation.1 | async-start | bytes 1048576 | tf_op jit(solution)/shard_map/all_to_all | solution.py:81
  53.0 114.0 %all-gather.7.cloned.1.call-start = ((), (), s32[]{:S(2)}) async-start(), calls=%async_computation.9 | async-start | bytes 2359296 | tf_op jit(solution)/shard_map/all_gather | solution.py:139
  53.8 151.5 %all-gather.5.cloned.1.call-start = ((), (), s32[]{:S(2)}) async-start(), calls=%async_computation.8 | async-start | bytes 8912896 | tf_op jit(solution)/shard_map/all_gather | solution.py:122
  146.9 4.9 %copy-start.7 = (f32[2048]{0:T(1024)S(1)}, f32[2048]{0:T(1024)}, u32[]{:S(2)}) copy-start(f32[2048]{0:T(1024)} %param.16) | copy-start | bytes 24580
  146.9 5.9 %copy-start.3 = (f32[64,2048]{1,0:T(8,128)S(1)}, f32[64,2048]{1,0:T(8,128)}, u32[]{:S(2)}) copy-start(f32[64,2048]{1,0:T(8,128)} %param.22) | copy-start | bytes 1572868
  146.9 6.7 %copy-start.4 = (f32[16,8192]{1,0:T(8,128)S(1)}, f32[16,8192]{1,0:T(8,128)}, u32[]{:S(2)}) copy-start(f32[16,8192]{1,0:T(8,128)} %param.21) | copy-start | bytes 1572868
  152.8 108.7 %all-gather.11.cloned.1.call-start = ((), (), s32[]{:S(2)}) async-start(), calls=%async_computation.11 | async-start | bytes 2359296 | tf_op jit(solution)/shard_map/all_gather | solution.py:145
  153.6 162.0 %all-gather.9.cloned.1.call-start = ((), (), s32[]{:S(2)}) async-start(), calls=%async_computation.10 | async-start | bytes 2359296 | tf_op jit(solution)/shard_map/all_gather | solution.py:140
  166.7 266.3 %reduce-scatter.2.cloned.1.call-start = ((), (), s32[]{:S(2)}) async-start(), calls=%async_computation.12 | async-start | bytes 8912896 | tf_op jit(solution)/shard_map/reduce_scatter | solution.py:146
  330.9 0.7 copy-start.8
Sparse Core Ops, SparseCore 0:
  56.2 54.2 all-gather.6
  152.9 52.3 all-gather.4
  208.2 53.2 all-gather.10
  263.7 51.8 all-gather.8
  331.0 101.9 reduce-scatter.1
where the time goes:
time: 443 us; the launch traced here: 442 us
  waiting for transfers between devices  240 us (54%)
  matrix products  88.8 us (20%)
  blocking collectives  43.3 us (10%)
  other arithmetic  21.6 us (5%)
  starting transfers between devices  18.7 us (4%)
  between operations  14.8 us (3%)
  local copies, waits for them, and re-layouts  12.2 us (3%)
    reduce_scatter x1, waiting for transfers between devices, on_device(): lax.psum_scatter(jnp.dot(activated, down_block, preferred_element_type=jn...  82.7 us
    all_gather x1, waiting for transfers between devices, on_device(): lax.all_gather(up_piece, 'dp', axis=0, tiled=True)  54.1 us
    all_gather x1, waiting for transfers between devices, on_device(): lax.all_gather(down_rows.astype(jnp.bfloat16), 'dp', axis=0, tiled=True)  45.8 us
    all_gather x1, waiting for transfers between devices, on_device(): mlp_group = lax.all_gather(mlp_in, 'mp', axis=0, tiled=True)  38.3 us
    sub x4, matrix products, attend_block(): expd = jnp.exp(scores - top)  28.7 us
    dot_general x4, matrix products, attend_block(): jnp.einsum('hts,sd->thd', weights, value_in, preferred_element_type=jnp.f...  19.4 us
    all_to_all x1, blocking collectives, on_device(): lax.all_to_all(page_send, 'dp', split_axis=0, concat_axis=0, tiled=True)  18 us
    dot_general x1, matrix products, on_device(): jnp.dot(activated, down_block, preferred_element_type=jnp.float32)  15.2 us
  transfers between devices with their start and end apart: 9, of which 7 were waited for; matrix products, arithmetic and copies ran while one was open for 23% of the time, Pallas kernels for 0%

commit v1 on v0

--- a/solution.py
+++ b/solution.py
@@ -119,7 +119,9 @@
     ).astype(jnp.bfloat16)
     hidden_f = hidden_state.astype(jnp.float32)
     mlp_in = rms_scale(hidden_f, mlp_gain).astype(jnp.bfloat16)
-    mlp_group = lax.all_gather(mlp_in, "mp", axis=0, tiled=True)
+    mlp_group = jnp.concatenate(
+        lax.all_to_all(jnp.stack([mlp_in] * lax.axis_size("mp")), "mp", 0, 0), axis=0
+    )
     rows_dev = gate_rows.shape[0]
     block_width = gate_rows.shape[1] // (dp_count * mp_count)
 

time: 443 us -> 429 us (0.968)
  blocking collectives: 43.3 us -> 18 us
  starting transfers between devices: 18.7 us -> 30.6 us
  waiting for transfers between devices: 240 us -> 232 us
  local copies, waits for them, and re-layouts: 12.2 us -> 19.7 us
    all_to_all x0 -> x3, waiting for transfers between devices: none -> 122 us  [the longest x1 110 us: on_device(): lax.all_to_all(jnp.stack([mlp_in] * lax.axis_size('mp')), 'mp', 0, 0)]
    all_gather x1, waiting for transfers between devices: 54.1 us -> 7.43 us  [on_device(): lax.all_gather(up_piece, 'dp', axis=0, tiled=True)]
    all_gather x1, waiting for transfers between devices: 45.8 us -> 0.01 us  [on_device(): lax.all_gather(down_rows.astype(jnp.bfloat16), 'dp', axis=0, tiled=True)]
    all_gather x1 -> x0, waiting for transfers between devices: 38.3 us -> none  [on_device(): mlp_group = lax.all_gather(mlp_in, 'mp', axis=0, tiled=True)]
    all_to_all x2 -> x0, blocking collectives: 25.3 us -> none  [the longest x1 13.5 us: on_device(): lax.all_to_all(attended, 'mp', split_axis=0, concat_axis=1, tiled=True)]
    all_to_all x0 -> x3, starting transfers between devices: none -> 12 us  [the longest x1 4.89 us: on_device(): lax.all_to_all(jnp.stack([mlp_in] * lax.axis_size('mp')), 'mp', 0, 0)]
  transfers between devices with their start and end apart: 9 -> 11, of which waited for: 7 -> 8; matrix products, arithmetic and copies ran while one was open for 23% -> 25% of each run, Pallas kernels for 0% -> 0%
where the time goes in v1:
time: 429 us; the launch traced here: 427 us
  waiting for transfers between devices  232 us (54%)
  matrix products  88.8 us (21%)
  starting transfers between devices  30.6 us (7%)
  other arithmetic  20.8 us (5%)
  local copies, waits for them, and re-layouts  19.7 us (5%)
  blocking collectives  18 us (4%)
  between operations  14.8 us (3%)
    all_to_all x1, waiting for transfers between devices, on_device(): lax.all_to_all(jnp.stack([mlp_in] * lax.axis_size('mp')), 'mp', 0, 0)  110 us
    reduce_scatter x1, waiting for transfers between devices, on_device(): lax.psum_scatter(jnp.dot(activated, down_block, preferred_element_type=jn...  82.4 us
    sub x4, matrix products, attend_block(): expd = jnp.exp(scores - top)  28.7 us
    dot_general x4, matrix products, attend_block(): jnp.einsum('hts,sd->thd', weights, value_in, preferred_element_type=jnp.f...  19.4 us
    all_to_all x1, blocking collectives, on_device(): lax.all_to_all(page_send, 'dp', split_axis=0, concat_axis=0, tiled=True)  18 us
    dot_general x1, matrix products, on_device(): jnp.dot(activated, down_block, preferred_element_type=jnp.float32)  15.2 us
    and x4, other arithmetic, attend_block(): (query_segment[:, None] == segment_all[None, :]) & (group_rows[None, :] <...  14.5 us
    dot_general x1, matrix products, on_device(): gate = jnp.dot(mlp_group, gate_block, preferred_element_type=jnp.float32)  10.5 us
  transfers between devices with their start and end apart: 11, of which 8 were waited for; matrix products, arithmetic and copies ran while one was open for 25% of the time, Pallas kernels for 0%

profile of v1, /device:TPU:4, one launch (start us, length us, event | category | flops | bytes accessed | tf_op | source)
XLA Modules:
  0.0 427.3 jit_solution(2582295379991983839)
XLA Ops:
  8.5 5.2 %all-to-all-start = ((bf16[128,16,1]{0,2,1:T(2,128)(2,1)}), bf16[128,16,1]{0,2,1:T(2,128)(2,1)S(1)}, u32[]{:S(2)}, u32[]{:S(2)}) async-start(bf16[128,16,1]{0,2,1:T(2,128)(2,1)} %broadcast_in_dim.28), calls=%async_computation | async-start | bytes 16384 | tf_op jit(solution)/shard_map/all_to_all | solution.py:83
  20.4 5.7 %all-to-all-start.5 = ((bf16[16,16,512]{2,0,1:T(8,128)(2,1)}), bf16[16,16,512]{2,0,1:T(8,128)(2,1)S(1)}, u32[]{:S(2)}, u32[]{:S(2)}) async-start(bf16[16,16,512]{2,0,1:T(8,128)(2,1)} %copy.77), calls=%async_computation.5 | async-start | bytes 524288 | tf_op jit(solution)/shard_map/all_to_all | solution.py:135
  26.3 7.8 %all-to-all-done.5 = bf16[16,16,512]{2,0,1:T(8,128)(2,1)S(1)} async-done(((bf16[16,16,512]{2,0,1:T(8,128)(2,1)}), bf16[16,16,512]{2,0,1:T(8,128)(2,1)S(1)}, u32[]{:S(2)}, u32[]{:S(2)}) %all-to-all-start.5) | async-done | bytes 262176 | tf_op jit(solution)/shard_map/all_to_all | solution.py:135
  38.7 6.8 %fusion.42 = f32[128,2048]{0,1:T(8,128)S(1)} fusion(bf16[2048,2048]{1,0:T(8,128)(2,1)} %param.17, bf16[128,2048]{1,0:T(8,128)(2,1)S(1)} %copy-done, f32[2048]{0:T(1024)S(1)} %copy-done.6, f32[128]{0:T(128)S(1)} %add_rsqrt_fusion.1), kind=kOutput, calls=%fused_computation.57 | convolution fusion | flops 1074790400 | bytes 9970176 | tf_op jit(solution)/shard_map/dot_general | solution.py:70
  55.4 8.5 %all-to-all-done.1 = bf16[128,16,128]{0,2,1:T(8,128)(2,1)S(1)} async-done(((bf16[128,16,128]{0,2,1:T(8,128)(2,1)}), bf16[128,16,128]{0,2,1:T(8,128)(2,1)S(1)}, u32[]{:S(2)}, u32[]{:S(2)}) %all-to-all-start.1) | async-done | bytes 524320 | tf_op jit(solution)/shard_map/all_to_all | solution.py:81
  64.5 71.2 %while.12 = (s32[]{:T(128)}, bf16[4,512,128]{2,1,0:T(8,128)(2,1)}, s32[4]{0:T(128)S(1)}, s32[2048]{0:T(1024)S(1)}, pred[2048]{0:T(1024)(128)(4,1)S(1)}, /*index=...) while((s32[]{:T(128)}, bf16[4,512,128]{2,1,0:T(8,128)(2,1)}, ...), condition=%wide.region_4.5_spmd.clone.clone, body=%wide.region_1.0_spmd.clone.clone.sunk | while | flops 555813376 | bytes 20214460 | solution.py:114
  69.5 7.2 %fusion.78 = (f32[2,512]{1,0:T(2,128)S(1)}, f32[2,512,2048]{2,1,0:T(8,128)}) fusion(pred[512,2048]{1,0:T(8,128)(4,1)S(1)} %fusion.77, bf16[2048,64]{0,1:T(8,128)(2,1)} %get-tuple-element.220, bf16[2048,2,64]{0,2,1:T(8,128)(2,1)S(1)} %get-tuple-element.219, s32[]{:T(128)S(6)} %select_n.41), kind=kOutput, calls=%fused_computation.76.clone.1 | convolution fusion | flops 276826112 | bytes 9834500 | tf_op jit(solution)/shard_map/while/body/eval_jaxpr/sub | solution.py:109
  76.6 4.9 %fusion.79 = bf16[2,512,64]{1,2,0:T(8,128)(2,1)S(1)} fusion(f32[2,512,2048]{2,1,0:T(8,128)} %get-tuple-element.188, f32[2,512]{1,0:T(2,128)S(1)} %get-tuple-element.189, bf16[2048,64]{0,1:T(8,128)(2,1)S(1)} %get-tuple-element.221), kind=kOutput, calls=%fused_computation.17.clone.1 | convolution fusion | flops 272695296 | bytes 8785920 | tf_op jit(solution)/shard_map/while/body/eval_jaxpr/hts,sd->thd/dot_general | solution.py:111
  87.3 7.2 %fusion.78 = (f32[2,512]{1,0:T(2,128)S(1)}, f32[2,512,2048]{2,1,0:T(8,128)}) fusion(pred[512,2048]{1,0:T(8,128)(4,1)S(1)} %fusion.77, bf16[2048,64]{0,1:T(8,128)(2,1)} %get-tuple-element.220, bf16[2048,2,64]{0,2,1:T(8,128)(2,1)S(1)} %get-tuple-element.219, s32[]{:T(128)S(6)} %select_n.41), kind=kOutput, calls=%fused_computation.76.clone.1 | convolution fusion | flops 276826112 | bytes 9834500 | tf_op jit(solution)/shard_map/while/body/eval_jaxpr/sub | solution.py:109
  94.5 4.9 %fusion.79 = bf16[2,512,64]{1,2,0:T(8,128)(2,1)S(1)} fusion(f32[2,512,2048]{2,1,0:T(8,128)} %get-tuple-element.188, f32[2,512]{1,0:T(2,128)S(1)} %get-tuple-element.189, bf16[2048,64]{0,1:T(8,128)(2,1)S(1)} %get-tuple-element.221), kind=kOutput, calls=%fused_computation.17.clone.1 | convolution fusion | flops 272695296 | bytes 8785920 | tf_op jit(solution)/shard_map/while/body/eval_jaxpr/hts,sd->thd/dot_general | solution.py:111
  105.1 7.2 %fusion.78 = (f32[2,512]{1,0:T(2,128)S(1)}, f32[2,512,2048]{2,1,0:T(8,128)}) fusion(pred[512,2048]{1,0:T(8,128)(4,1)S(1)} %fusion.77, bf16[2048,64]{0,1:T(8,128)(2,1)} %get-tuple-element.220, bf16[2048,2,64]{0,2,1:T(8,128)(2,1)S(1)} %get-tuple-element.219, s32[]{:T(128)S(6)} %select_n.41), kind=kOutput, calls=%fused_computation.76.clone.1 | convolution fusion | flops 276826112 | bytes 9834500 | tf_op jit(solution)/shard_map/while/body/eval_jaxpr/sub | solution.py:109
  112.3 4.8 %fusion.79 = bf16[2,512,64]{1,2,0:T(8,128)(2,1)S(1)} fusion(f32[2,512,2048]{2,1,0:T(8,128)} %get-tuple-element.188, f32[2,512]{1,0:T(2,128)S(1)} %get-tuple-element.189, bf16[2048,64]{0,1:T(8,128)(2,1)S(1)} %get-tuple-element.221), kind=kOutput, calls=%fused_computation.17.clone.1 | convolution fusion | flops 272695296 | bytes 8785920 | tf_op jit(solution)/shard_map/while/body/eval_jaxpr/hts,sd->thd/dot_general | solution.py:111
  122.9 7.2 %fusion.78 = (f32[2,512]{1,0:T(2,128)S(1)}, f32[2,512,2048]{2,1,0:T(8,128)}) fusion(pred[512,2048]{1,0:T(8,128)(4,1)S(1)} %fusion.77, bf16[2048,64]{0,1:T(8,128)(2,1)} %get-tuple-element.220, bf16[2048,2,64]{0,2,1:T(8,128)(2,1)S(1)} %get-tuple-element.219, s32[]{:T(128)S(6)} %select_n.41), kind=kOutput, calls=%fused_computation.76.clone.1 | convolution fusion | flops 276826112 | bytes 9834500 | tf_op jit(solution)/shard_map/while/body/eval_jaxpr/sub | solution.py:109
  130.1 4.8 %fusion.79 = bf16[2,512,64]{1,2,0:T(8,128)(2,1)S(1)} fusion(f32[2,512,2048]{2,1,0:T(8,128)} %get-tuple-element.188, f32[2,512]{1,0:T(2,128)S(1)} %get-tuple-element.189, bf16[2048,64]{0,1:T(8,128)(2,1)S(1)} %get-tuple-element.221), kind=kOutput, calls=%fused_computation.17.clone.1 | convolution fusion | flops 272695296 | bytes 8785920 | tf_op jit(solution)/shard_map/while/body/eval_jaxpr/hts,sd->thd/dot_general | solution.py:111
  141.2 8.9 %all-to-all-done.3 = bf16[16,128,128]{2,1,0:T(8,128)(2,1)S(1)} async-done(((bf16[16,128,128]{2,1,0:T(8,128)(2,1)}), bf16[16,128,128]{2,1,0:T(8,128)(2,1)S(1)}, u32[]{:S(2)}, u32[]{:S(2)}) %all-to-all-start.3) | async-done | bytes 524320 | tf_op jit(solution)/shard_map/all_to_all | solution.py:116
  154.0 4.7 %multiply_reduce_fusion = (f32[128]{0:T(128)S(1)}, f32[128,2048]{1,0:T(8,128)S(1)}) fusion(bf16[128,2048]{0,1:T(8,128)(2,1)S(1)} %bitcast.113, bf16[2048,2048]{1,0:T(8,128)(2,1)} %param.19, bf16[128,2048]{1,0:T(8,128)(2,1)S(1)} %copy-done), kind=kOutput, calls=%fused_computation.44 | convolution fusion | flops 1075314560 | bytes 10486272 | tf_op jit(solution)/shard_map/dot_general | solution.py:118
  161.7 4.3 %stack.2 = bf16[16,128,2048]{2,1,0:T(8,128)(2,1)} broadcast(bf16[128,2048]{1,0:T(8,128)(2,1)S(1)} %multiply_convert_fusion.1), dimensions={1,2} | broadcast | bytes 8912896 | tf_op jit(solution)/shard_map/stack | solution.py:123
  166.0 4.9 %all-to-all-start.4 = ((bf16[16,128,2048]{2,1,0:T(8,128)(2,1)}), bf16[16,128,2048]{2,1,0:T(8,128)(2,1)}, u32[]{:S(2)}, u32[]{:S(2)}) async-start(bf16[16,128,2048]{2,1,0:T(8,128)(2,1)} %stack.2), calls=%async_computation.4 | async-start | bytes 16777216 | tf_op jit(solution)/shard_map/all_to_all | solution.py:123
  172.7 110.3 %all-to-all-done.4 = bf16[16,128,2048]{2,1,0:T(8,128)(2,1)} async-done(((bf16[16,128,2048]{2,1,0:T(8,128)(2,1)}), bf16[16,128,2048]{2,1,0:T(8,128)(2,1)}, u32[]{:S(2)}, u32[]{:S(2)}) %all-to-all-start.4) | async-done | bytes 8388640 | tf_op jit(solution)/shard_map/all_to_all | solution.py:123
  283.0 10.5 %fusion.57 = f32[2048,512]{1,0:T(8,128)} fusion(bf16[2048,2048]{1,0:T(8,128)(2,1)} %bitcast.21, bf16[2048,512]{1,0:T(8,128)(2,1)} %all-gather.4.cloned.1.call-done), kind=kOutput, calls=%fused_computation.77 | convolution fusion | flops 4294967296 | bytes 14680064 | tf_op jit(solution)/shard_map/dot_general | solution.py:144
  293.4 7.4 %all-gather.6.cloned.1.call-done = bf16[2048,512]{1,0:T(8,128)(2,1)} async-done(((bf16[256,512]{1,0:T(8,128)(2,1)}), bf16[2048,512]{1,0:T(8,128)(2,1)}) %all-gather.6.cloned.1.call-update) | async-done | bytes 2097168 | tf_op jit(solution)/shard_map/all_gather | solution.py:142
  300.9 15.2 %convolution_convert_fusion.1 = bf16[2048,2048]{1,0:T(8,128)(2,1)} fusion(bf16[512,2048]{1,0:T(8,128)(2,1)} %all-gather.8.cloned.1.call-done, f32[2048,512]{1,0:T(8,128)} %fusion.57, bf16[2048,2048]{1,0:T(8,128)(2,1)} %bitcast.21, bf16[2048,512]{1,0:T(8,128)(2,1)} %all-gather.6.cloned.1.call-done), kind=kOutput, calls=%fused_computation.32 | convolution fusion | flops 8600420352 | bytes 25165824 | tf_op jit(solution)/shard_map/dot_general | solution.py:149
  317.6 18.0 %all_to_all.101 = bf16[8,2,16,1024]{3,2,1,0:T(8,128)(2,1)S(1)} all-to-all(bf16[8,2,16,1024]{3,2,1,0:T(8,128)(2,1)S(1)} %bitcast.121), channel_id=1, replica_groups=mesh['dp'=8,'mp'=16] {'dp'}, dimensions={0} | all-to-all | bytes 1048576 | tf_op jit(solution)/shard_map/all_to_all | solution.py:172
  335.6 82.4 %reduce-scatter.2.cloned.1.call-done = bf16[128,2048]{1,0:T(8,128)(2,1)} async-done(((bf16[2048,2048]{1,0:T(8,128)(2,1)}), bf16[128,2048]{1,0:T(8,128)(2,1)}) %reduce-scatter.2.cloned.1.call-update) | async-done | bytes 524304 | tf_op jit(solution)/shard_map/reduce_scatter | solution.py:148
  (110 shorter events, 60.9 us)
Async XLA Ops:
  7.2 11.3 %copy-start.3 = (f32[16,8192]{1,0:T(8,128)S(1)}, f32[16,8192]{1,0:T(8,128)}, u32[]{:S(2)}) copy-start(f32[16,8192]{1,0:T(8,128)} %param.20) | copy-start | bytes 1572868
  8.5 11.9 %all-to-all-start = ((bf16[128,16,1]{0,2,1:T(2,128)(2,1)}), bf16[128,16,1]{0,2,1:T(2,128)(2,1)S(1)}, u32[]{:S(2)}, u32[]{:S(2)}) async-start(bf16[128,16,1]{0,2,1:T(2,128)(2,1)} %broadcast_in_dim.28), calls=%async_computation | async-start | bytes 16384 | tf_op jit(solution)/shard_map/all_to_all | solution.py:83
  18.3 20.3 %copy-start = (bf16[128,2048]{1,0:T(8,128)(2,1)S(1)}, bf16[128,2048]{1,0:T(8,128)(2,1)}, u32[]{:S(2)}) copy-start(bf16[128,2048]{1,0:T(8,128)(2,1)} %param.14) | copy-start | bytes 1572868
  18.3 20.3 %copy-start.6 = (f32[2048]{0:T(1024)S(1)}, f32[2048]{0:T(1024)}, u32[]{:S(2)}) copy-start(f32[2048]{0:T(1024)} %param.15) | copy-start | bytes 24580
  20.4 13.8 %all-to-all-start.5 = ((bf16[16,16,512]{2,0,1:T(8,128)(2,1)}), bf16[16,16,512]{2,0,1:T(8,128)(2,1)S(1)}, u32[]{:S(2)}, u32[]{:S(2)}) async-start(bf16[16,16,512]{2,0,1:T(8,128)(2,1)} %copy.77), calls=%async_computation.5 | async-start | bytes 524288 | tf_op jit(solution)/shard_map/all_to_all | solution.py:135
  34.1 11.3 %copy-start.1 = (bf16[16,16,512]{2,0,1:T(8,128)(2,1)}, bf16[16,16,512]{2,0,1:T(8,128)(2,1)S(1)}, u32[]{:S(2)}) copy-start(bf16[16,16,512]{2,0,1:T(8,128)(2,1)S(1)} %all-to-all-done.5) | copy-start | bytes 786436
  35.1 14.4 %all-to-all-start.2 = ((bf16[128,16,128]{0,2,1:T(8,128)(2,1)}), bf16[128,16,128]{0,2,1:T(8,128)(2,1)S(1)}, u32[]{:S(2)}, u32[]{:S(2)}) async-start(bf16[128,16,128]{0,2,1:T(8,128)(2,1)} %bitcast.10), calls=%async_computation.2 | async-start | bytes 1048576 | tf_op jit(solution)/shard_map/all_to_all | solution.py:82
  49.5 14.4 %all-to-all-start.1 = ((bf16[128,16,128]{0,2,1:T(8,128)(2,1)}), bf16[128,16,128]{0,2,1:T(8,128)(2,1)S(1)}, u32[]{:S(2)}, u32[]{:S(2)}) async-start(bf16[128,16,128]{0,2,1:T(8,128)(2,1)} %bitcast.5), calls=%async_computation.1 | async-start | bytes 1048576 | tf_op jit(solution)/shard_map/all_to_all | solution.py:81
  53.0 119.7 %all-gather.4.cloned.1.call-start = ((), (), s32[]{:S(2)}) async-start(), calls=%async_computation.9 | async-start | bytes 2359296 | tf_op jit(solution)/shard_map/all_gather | solution.py:141
  64.5 74.8 %copy-start.4 = (f32[16,8192]{1,0:T(8,128)S(1)}, f32[16,8192]{1,0:T(8,128)}, u32[]{:S(2)}) copy-start(f32[16,8192]{1,0:T(8,128)} %param.21) | copy-start | bytes 1572868
  135.7 14.4 %all-to-all-start.3 = ((bf16[16,128,128]{2,1,0:T(8,128)(2,1)}), bf16[16,128,128]{2,1,0:T(8,128)(2,1)S(1)}, u32[]{:S(2)}, u32[]{:S(2)}) async-start(bf16[16,128,128]{2,1,0:T(8,128)(2,1)} %bitcast.126), calls=%async_computation.3 | async-start | bytes 1048576 | tf_op jit(solution)/shard_map/all_to_all | solution.py:116
  150.1 11.6 %all-to-all-start.6 = ((bf16[16,16,512]{2,0,1:T(8,128)(2,1)}), bf16[16,16,512]{2,0,1:T(8,128)(2,1)S(1)}, u32[]{:S(2)}, u32[]{:S(2)}) async-start(bf16[16,16,512]{2,0,1:T(8,128)(2,1)} %copy.79), calls=%async_computation.6 | async-start | bytes 524288 | tf_op jit(solution)/shard_map/all_to_all | solution.py:136
  153.9 4.8 %copy-start.7 = (f32[2048]{0:T(1024)S(1)}, f32[2048]{0:T(1024)}, u32[]{:S(2)}) copy-start(f32[2048]{0:T(1024)} %param.16) | copy-start | bytes 24580
  161.7 4.3 %copy-start.2 = (bf16[16,16,512]{2,0,1:T(8,128)(2,1)}, bf16[16,16,512]{2,0,1:T(8,128)(2,1)S(1)}, u32[]{:S(2)}) copy-start(bf16[16,16,512]{2,0,1:T(8,128)(2,1)S(1)} %all-to-all-done.6) | copy-start | bytes 786436
  166.0 5.0 %copy-start.5 = (f32[64,2048]{1,0:T(8,128)S(1)}, f32[64,2048]{1,0:T(8,128)}, u32[]{:S(2)}) copy-start(f32[64,2048]{1,0:T(8,128)} %param.22) | copy-start | bytes 1572868
  166.0 117.0 %all-to-all-start.4 = ((bf16[16,128,2048]{2,1,0:T(8,128)(2,1)}), bf16[16,128,2048]{2,1,0:T(8,128)(2,1)}, u32[]{:S(2)}, u32[]{:S(2)}) async-start(bf16[16,128,2048]{2,1,0:T(8,128)(2,1)} %stack.2), calls=%async_computation.4 | async-start | bytes 16777216 | tf_op jit(solution)/shard_map/all_to_all | solution.py:123
  170.9 122.6 %all-gather.8.cloned.1.call-start = ((), (), s32[]{:S(2)}) async-start(), calls=%async_computation.11 | async-start | bytes 2359296 | tf_op jit(solution)/shard_map/all_gather | solution.py:147
  171.7 129.2 %all-gather.6.cloned.1.call-start = ((), (), s32[]{:S(2)}) async-start(), calls=%async_computation.10 | async-start | bytes 2359296 | tf_op jit(solution)/shard_map/all_gather | solution.py:142
  172.4 245.6 %reduce-scatter.2.cloned.1.call-start = ((), (), s32[]{:S(2)}) async-start(), calls=%async_computation.12 | async-start | bytes 8912896 | tf_op jit(solution)/shard_map/reduce_scatter | solution.py:148
  316.1 0.7 copy-start.8
Sparse Core Ops, SparseCore 0:
  56.2 54.2 all-gather.3
  174.6 68.3 all-gather.7
  246.0 54.8 all-gather.5
  316.3 101.7 reduce-scatter.1
